TPU v7x, 512 devices: a whole 4x8x8 slice. The times are simulated.
512 devices in a mesh: aux: 32 (over x_lo, y, core), pair: 16 (over z, x_hi).
Axes of the slice: x: 4 (x_hi: 2, x_lo: 2; x = x_hi * 2 + x_lo), y: 8, z: 8, core: 2. Of those that a mesh axis runs over, the one named last changes fastest.
Arguments:
- integrals: bfloat16 [4096, 32, 512], P('aux', 'pair'), may hold values from -0.5 to 0.5
- occ_density: bfloat16 [32, 32], replicated, may hold values from -1 to 1
- virt_density: bfloat16 [512, 512], replicated, may hold values from -0.25 to 0.25
- screen: int32 [64, 32], P('aux', 'pair'), may hold values 0 or 1
Outputs:
- polar: float32 [4096, 4096], P('aux', 'pair')
All inputs are finite; a program needn't handle non-finite values. No bound on the sum of `screen` on one device may be relied on, other than what follows from the above.
Results may differ from a plain program's by a relative error of at most 0.0041.
Values may be sent and summed in bfloat16 or wider, within the bound.
No kernel may reach another device: no remote copies, remote signals or barrier semaphores. Data moves between devices by JAX's collectives and lax.ppermute only.
A program may use at most 64 MiB of HBM per device.

v0:
```python
import jax
import jax.numpy as jnp
from jax import lax
from jax.sharding import Mesh, PartitionSpec as P

AUX = ("x_lo", "y", "core")
PAIR = ("z", "x_hi")
PLANE = ("x_lo", "core", "z", "x_hi")
WIDE = ("x_lo", "core", "x_hi")


def exchange(values):
    pieces = values.reshape(2, 2, 2, 16, 2, 8, 64)
    pieces = pieces.transpose(0, 1, 5, 2, 3, 4, 6).reshape(64, 16, 128)
    got = lax.all_to_all(pieces, PLANE, 0, 0, tiled=True)
    got = got.reshape(4, 16, 16, 128).transpose(0, 2, 1, 3)
    return got.reshape(64, 2048)


def body(integrals, occ_density, virt_density, screen):
    aux_rows, local_pairs, orbitals = integrals.shape
    blocks = screen.shape[0]
    grouped = integrals.reshape(blocks, aux_rows // blocks, local_pairs, orbitals)
    screened = jnp.where(screen[:, None, :, None] > 0, grouped, jnp.zeros_like(grouped)).reshape(
        aux_rows, local_pairs, orbitals
    )
    virtual = (
        jnp.dot(
            screened.reshape(aux_rows * local_pairs, orbitals),
            virt_density,
            preferred_element_type=jnp.float32,
        )
        .astype(jnp.bfloat16)
        .reshape(aux_rows, local_pairs, orbitals)
    )
    mine = exchange(screened)
    columns = lax.all_gather(mine, "y", axis=0, tiled=True)
    virt_rows = exchange(virtual).reshape(64, 32, 64)
    occupied = jnp.einsum("pms,ml->pls", virt_rows, occ_density, preferred_element_type=jnp.float32)
    occupied = occupied.astype(jnp.bfloat16).reshape(64, 2048)
    rows = lax.all_gather(occupied, WIDE, axis=0, tiled=True)
    rows = rows.reshape(8, 4, 16, 2048).transpose(1, 0, 2, 3).reshape(512, 2048)
    part = lax.dot_general(
        columns, rows, (((1,), (1,)), ((), ())), preferred_element_type=jnp.float32
    )
    part = part.astype(jnp.bfloat16)
    tiles = part.reshape(4, 2, 2, 32, 2, 2, 128).transpose(4, 5, 2, 0, 1, 3, 6).reshape(64, 32, 128)
    got = lax.all_to_all(tiles, PLANE, 0, 0, tiled=True)
    total = jnp.sum(got.reshape(2, 2, 8, 2, 2, 16, 128).astype(jnp.float32), axis=2)
    return total.transpose(5, 3, 0, 1, 2, 4).reshape(128, 256)


def solution(mesh):
    fine = Mesh(mesh.devices.reshape(2, 8, 2, 8, 2), AUX + PAIR)
    placed = (P(AUX, PAIR, None), P(), P(), P(AUX, PAIR))
    return jax.shard_map(body, mesh=fine, in_specs=placed, out_specs=P(AUX, PAIR), check_vma=False)
```

profile of v0, /device:TPU:6, one launch (start us, length us, event | category | flops | bytes accessed | tf_op | source)
XLA Modules:
  0.0 188.4 jit_solution(10271872201832409334)
XLA Ops:
  6.5 0.7 broadcast_compare_fusion
  7.3 0.1 broadcast_in_dim.23
  7.4 1.1 reshape.50
  8.5 0.3 convolution_convert_fusion.2
  8.9 0.3 reshape_reshape.8
  9.2 0.5 copy.36
  9.7 0.3 reshape.51
  10.0 26.7 %all_to_all.15 = bf16[64,16,128]{2,1,0:T(8,128)(2,1)S(1)} all-to-all(bf16[64,16,128]{2,1,0:T(8,128)(2,1)S(1)} %reshape.51), channel_id=1, replica_groups=mesh['x_lo'=2,'y'=8,'core'=2,'z'=8,'x_hi'=2] {'x_lo','core','z','x_hi'}, dimensions={0} | all-to-all | bytes 524288 | tf_op jit(solution)/shard_map/all_to_all | solution.py:15
  36.7 0.2 reshape_reshape.9
  37.0 0.3 fusion
  37.3 1.2 reshape.53
  38.6 0.3 reshape.46
  39.0 0.6 fusion.1
  39.5 0.3 reshape.47
  39.8 17.9 %all_to_all.16 = bf16[64,16,128]{2,1,0:T(8,128)(2,1)S(1)} all-to-all(bf16[64,16,128]{2,1,0:T(8,128)(2,1)S(1)} %reshape.47), channel_id=1, replica_groups=mesh['x_lo'=2,'y'=8,'core'=2,'z'=8,'x_hi'=2] {'x_lo','core','z','x_hi'}, dimensions={0} | all-to-all | bytes 524288 | tf_op jit(solution)/shard_map/all_to_all | solution.py:15
  57.8 0.8 copy.37
  58.6 36.2 %all-gather.5.cloned.1.call-done = bf16[512,2048]{1,0:T(8,128)(2,1)} async-done(((bf16[64,2048]{1,0:T(8,128)(2,1)}), bf16[512,2048]{1,0:T(8,128)(2,1)}) %all-gather.5.cloned.1.call-update) | async-done | bytes 2097168 | tf_op jit(solution)/shard_map/all_gather | solution.py:41
  94.9 1.7 copy.26
  96.6 51.8 %all-gather.3.cloned.1.call-done = bf16[512,2048]{1,0:T(8,128)(2,1)} async-done(((bf16[64,2048]{1,0:T(8,128)(2,1)}), bf16[512,2048]{1,0:T(8,128)(2,1)}) %all-gather.3.cloned.1.call-update) | async-done | bytes 2097168 | tf_op jit(solution)/shard_map/all_gather | solution.py:37
  148.4 2.9 %convolution_convert_fusion = bf16[512,512]{1,0:T(8,128)(2,1)S(1)} fusion(bf16[512,2048]{1,0:T(8,128)(2,1)} %all-gather.3.cloned.1.call-done, bf16[512,2048]{1,0:T(8,128)(2,1)S(1)} %bitcast.39), kind=kOutput, calls=%fused_computation | convolution fusion | flops 1074003968 | bytes 4718592 | tf_op jit(solution)/shard_map/dot_general | solution.py:43
  151.2 0.1 reshape.56
  151.4 0.1 copy.27
  151.5 29.3 %all_to_all.17 = bf16[64,32,128]{2,1,0:T(8,128)(2,1)S(1)} all-to-all(bf16[64,32,128]{2,1,0:T(8,128)(2,1)S(1)} %bitcast.41), channel_id=1, replica_groups=mesh['x_lo'=2,'y'=8,'core'=2,'z'=8,'x_hi'=2] {'x_lo','core','z','x_hi'}, dimensions={0} | all-to-all | bytes 1048576 | tf_op jit(solution)/shard_map/all_to_all | solution.py:48
  180.8 0.8 copy.29
  (15 shorter events, 0.3 us)
Async XLA Ops:
  6.5 2.0 %copy-start = (bf16[512,512]{1,0:T(8,128)(2,1)S(1)}, bf16[512,512]{1,0:T(8,128)(2,1)}, u32[]{:S(2)}) copy-start(bf16[512,512]{1,0:T(8,128)(2,1)} %param.6) | copy-start | bytes 1572868
  6.5 88.3 %all-gather.5.cloned.1.call-start = ((), (), s32[]{:S(2)}) async-start(), calls=%async_computation.4 | async-start | bytes 2359296 | tf_op jit(solution)/shard_map/all_gather | solution.py:41
  8.9 28.1 %copy-start.2 = (bf16[32,32]{1,0:T(8,128)(2,1)S(1)}, bf16[32,32]{1,0:T(8,128)(2,1)}, u32[]{:S(2)}) copy-start(bf16[32,32]{1,0:T(8,128)(2,1)} %param.5) | copy-start | bytes 6148
  10.0 28.6 %copy-start.1 = (bf16[128,2,512]{2,1,0:T(2,128)(2,1)S(1)}, bf16[128,2,512]{2,1,0:T(2,128)(2,1)}, u32[]{:S(2)}) copy-start(bf16[128,2,512]{2,1,0:T(2,128)(2,1)} %param.4) | copy-start | bytes 786436
  38.6 109.8 %all-gather.3.cloned.1.call-start = ((), (), s32[]{:S(2)}) async-start(), calls=%async_computation.3 | async-start | bytes 2359296 | tf_op jit(solution)/shard_map/all_gather | solution.py:37
Sparse Core Ops, SparseCore 0:
  38.7 56.1 all-gather.4
  96.9 51.3 all-gather.2
where the time goes:
time: 189 us; the launch traced here: 188 us
  waiting for transfers between devices  88 us (47%)
  blocking collectives  73.9 us (39%)
  between operations  13.6 us (7%)
  local copies, waits for them, and re-layouts  7.99 us (4%)
  matrix products  3.54 us (2%)
    all_gather x1, waiting for transfers between devices, body(): columns = lax.all_gather(mine, 'y', axis=0, tiled=True)  51.8 us
    all_to_all x2, blocking collectives, exchange(): got = lax.all_to_all(pieces, PLANE, 0, 0, tiled=True)  44.6 us
    all_gather x1, waiting for transfers between devices, body(): rows = lax.all_gather(occupied, WIDE, axis=0, tiled=True)  36.2 us
    all_to_all x1, blocking collectives, body(): got = lax.all_to_all(tiles, PLANE, 0, 0, tiled=True)  29.3 us
  transfers between devices with their start and end apart: 2, of which 2 were waited for; matrix products, arithmetic and copies ran while one was open for 2% of the time, Pallas kernels for 0%

commit v1 on v0

--- a/solution.py
+++ b/solution.py
@@ -34,7 +34,9 @@
         .reshape(aux_rows, local_pairs, orbitals)
     )
     mine = exchange(screened)
-    columns = lax.all_gather(mine, "y", axis=0, tiled=True)
+    columns = jnp.concatenate(
+        lax.all_to_all(jnp.stack([mine] * lax.axis_size("y")), "y", 0, 0), axis=0
+    )
     virt_rows = exchange(virtual).reshape(64, 32, 64)
     occupied = jnp.einsum("pms,ml->pls", virt_rows, occ_density, preferred_element_type=jnp.float32)
     occupied = occupied.astype(jnp.bfloat16).reshape(64, 2048)

time: 189 us -> 162 us (0.86)
  blocking collectives: 73.9 us -> 34 us
  starting transfers between devices: 0.04 us -> 26.6 us
  waiting for transfers between devices: 88 us -> 70.5 us
  local copies, waits for them, and re-layouts: 7.99 us -> 11.7 us
    all_gather x1 -> x0, waiting for transfers between devices: 51.8 us -> none  [body(): columns = lax.all_gather(mine, 'y', axis=0, tiled=True)]
    all_to_all x2 -> x0, blocking collectives: 44.6 us -> none  [exchange(): got = lax.all_to_all(pieces, PLANE, 0, 0, tiled=True)]
    all_to_all x0 -> x3, starting transfers between devices: none -> 26.5 us  [the longest x2 19.4 us: exchange(): got = lax.all_to_all(pieces, PLANE, 0, 0, tiled=True)]
    all_to_all x0 -> x3, waiting for transfers between devices: none -> 23 us  [the longest x2 23 us: exchange(): got = lax.all_to_all(pieces, PLANE, 0, 0, tiled=True)]
    all_gather x1, waiting for transfers between devices: 36.2 us -> 47.4 us  [body(): rows = lax.all_gather(occupied, WIDE, axis=0, tiled=True)]
    all_to_all x1, blocking collectives: 29.3 us -> 34 us  [body(): got = lax.all_to_all(tiles, PLANE, 0, 0, tiled=True)]
  transfers between devices with their start and end apart: 2 -> 4, of which waited for: 2 -> 3; matrix products, arithmetic and copies ran while one was open for 2% -> 4% of each run, Pallas kernels for 0% -> 0%
where the time goes in v1:
time: 162 us; the launch traced here: 161 us
  waiting for transfers between devices  70.5 us (44%)
  blocking collectives  34 us (21%)
  starting transfers between devices  26.6 us (16%)
  between operations  13.6 us (8%)
  local copies, waits for them, and re-layouts  11.7 us (7%)
  matrix products  3.54 us (2%)
    all_gather x1, waiting for transfers between devices, body(): rows = lax.all_gather(occupied, WIDE, axis=0, tiled=True)  47.4 us
    all_to_all x1, blocking collectives, body(): got = lax.all_to_all(tiles, PLANE, 0, 0, tiled=True)  34 us
    all_to_all x2, waiting for transfers between devices, exchange(): got = lax.all_to_all(pieces, PLANE, 0, 0, tiled=True)  23 us
    all_to_all x2, starting transfers between devices, exchange(): got = lax.all_to_all(pieces, PLANE, 0, 0, tiled=True)  19.4 us
    all_to_all x1, starting transfers between devices, body(): lax.all_to_all(jnp.stack([mine] * lax.axis_size('y')), 'y', 0, 0)  7.12 us
  transfers between devices with their start and end apart: 4, of which 3 were waited for; matrix products, arithmetic and copies ran while one was open for 4% of the time, Pallas kernels for 0%

profile of v1, /device:TPU:6, one launch (start us, length us, event | category | flops | bytes accessed | tf_op | source)
XLA Modules:
  0.0 161.3 jit_solution(2917957493650729534)
XLA Ops:
  6.5 0.8 broadcast_compare_fusion
  7.3 1.3 reshape.48
  8.6 0.6 fusion.1
  9.2 0.9 reshape.49
  10.2 13.9 %all-to-all-start = ((bf16[64,16,128]{2,1,0:T(8,128)(2,1)}), bf16[64,16,128]{2,1,0:T(8,128)(2,1)S(1)}, u32[]{:S(2)}, u32[]{:S(2)}) async-start(bf16[64,16,128]{2,1,0:T(8,128)(2,1)} %reshape.49), calls=%async_computation | async-start | bytes 524288 | tf_op jit(solution)/shard_map/all_to_all | solution.py:15
  24.2 0.1 broadcast_in_dim.23
  24.4 0.3 convolution_convert_fusion.2
  24.7 0.3 reshape_reshape.8
  25.0 0.5 copy.36
  25.6 1.0 reshape.53
  26.5 10.4 %all-to-all-done = bf16[64,16,128]{2,1,0:T(8,128)(2,1)S(1)} async-done(((bf16[64,16,128]{2,1,0:T(8,128)(2,1)}), bf16[64,16,128]{2,1,0:T(8,128)(2,1)S(1)}, u32[]{:S(2)}, u32[]{:S(2)}) %all-to-all-start) | async-done | bytes 262176 | tf_op jit(solution)/shard_map/all_to_all | solution.py:15
  36.9 5.5 %all-to-all-start.2 = ((bf16[64,16,128]{2,1,0:T(8,128)(2,1)}), bf16[64,16,128]{2,1,0:T(8,128)(2,1)S(1)}, u32[]{:S(2)}, u32[]{:S(2)}) async-start(bf16[64,16,128]{2,1,0:T(8,128)(2,1)} %reshape.53), calls=%async_computation.2 | async-start | bytes 524288 | tf_op jit(solution)/shard_map/all_to_all | solution.py:15
  42.6 12.6 %all-to-all-done.2 = bf16[64,16,128]{2,1,0:T(8,128)(2,1)S(1)} async-done(((bf16[64,16,128]{2,1,0:T(8,128)(2,1)}), bf16[64,16,128]{2,1,0:T(8,128)(2,1)S(1)}, u32[]{:S(2)}, u32[]{:S(2)}) %all-to-all-start.2) | async-done | bytes 262176 | tf_op jit(solution)/shard_map/all_to_all | solution.py:15
  55.3 0.2 reshape_reshape.9
  55.6 0.3 fusion
  55.9 1.2 reshape.55
  57.1 1.6 stack.3
  58.7 7.1 %all-to-all-start.1 = ((bf16[8,64,2048]{2,1,0:T(8,128)(2,1)}), bf16[8,64,2048]{2,1,0:T(8,128)(2,1)S(1)}, u32[]{:S(2)}, u32[]{:S(2)}) async-start(bf16[8,64,2048]{2,1,0:T(8,128)(2,1)} %stack.3), calls=%async_computation.1 | async-start | bytes 4194304 | tf_op jit(solution)/shard_map/all_to_all | solution.py:38
  65.8 47.4 %all-gather.2.cloned.1.call-done = bf16[512,2048]{1,0:T(8,128)(2,1)} async-done(((bf16[64,2048]{1,0:T(8,128)(2,1)}), bf16[512,2048]{1,0:T(8,128)(2,1)}) %all-gather.2.cloned.1.call-update) | async-done | bytes 2097168 | tf_op jit(solution)/shard_map/all_gather | solution.py:43
  113.3 3.2 %copy.26 = bf16[4,8,16,2048]{3,2,1,0:T(8,128)(2,1)} copy(bf16[4,8,16,2048]{3,2,0,1:T(8,128)(2,1)} %bitcast.39) | data formatting | bytes 4194304 | tf_op jit(solution)/shard_map/transpose | solution.py:44
  116.4 2.9 %convolution_convert_fusion = bf16[512,512]{1,0:T(8,128)(2,1)S(1)} fusion(bf16[512,2048]{1,0:T(8,128)(2,1)S(1)} %bitcast.40, bf16[512,2048]{1,0:T(8,128)(2,1)} %bitcast.41), kind=kOutput, calls=%fused_computation | convolution fusion | flops 1074003968 | bytes 4718592 | tf_op jit(solution)/shard_map/dot_general | solution.py:45
  119.3 0.1 reshape.58
  119.5 34.0 %all_to_all.20 = bf16[64,32,128]{2,1,0:T(8,128)(2,1)S(1)} all-to-all(bf16[64,32,128]{2,1,0:T(8,128)(2,1)S(1)} %bitcast.43), channel_id=1, replica_groups=mesh['x_lo'=2,'y'=8,'core'=2,'z'=8,'x_hi'=2] {'x_lo','core','z','x_hi'}, dimensions={0} | all-to-all | bytes 1048576 | tf_op jit(solution)/shard_map/all_to_all | solution.py:50
  153.7 0.8 copy.29
  (17 shorter events, 0.6 us)
Async XLA Ops:
  6.5 17.8 %copy-start = (bf16[512,512]{1,0:T(8,128)(2,1)S(1)}, bf16[512,512]{1,0:T(8,128)(2,1)}, u32[]{:S(2)}) copy-start(bf16[512,512]{1,0:T(8,128)(2,1)} %param.6) | copy-start | bytes 1572868
  6.5 17.5 %copy-start.1 = (bf16[128,2,512]{2,1,0:T(2,128)(2,1)S(1)}, bf16[128,2,512]{2,1,0:T(2,128)(2,1)}, u32[]{:S(2)}) copy-start(bf16[128,2,512]{2,1,0:T(2,128)(2,1)} %param.4) | copy-start | bytes 786436
  10.2 26.8 %all-to-all-start = ((bf16[64,16,128]{2,1,0:T(8,128)(2,1)}), bf16[64,16,128]{2,1,0:T(8,128)(2,1)S(1)}, u32[]{:S(2)}, u32[]{:S(2)}) async-start(bf16[64,16,128]{2,1,0:T(8,128)(2,1)} %reshape.49), calls=%async_computation | async-start | bytes 524288 | tf_op jit(solution)/shard_map/all_to_all | solution.py:15
  25.5 30.0 %copy-start.2 = (bf16[32,32]{1,0:T(8,128)(2,1)S(1)}, bf16[32,32]{1,0:T(8,128)(2,1)}, u32[]{:S(2)}) copy-start(bf16[32,32]{1,0:T(8,128)(2,1)} %param.5) | copy-start | bytes 6148
  36.9 18.3 %all-to-all-start.2 = ((bf16[64,16,128]{2,1,0:T(8,128)(2,1)}), bf16[64,16,128]{2,1,0:T(8,128)(2,1)S(1)}, u32[]{:S(2)}, u32[]{:S(2)}) async-start(bf16[64,16,128]{2,1,0:T(8,128)(2,1)} %reshape.53), calls=%async_computation.2 | async-start | bytes 524288 | tf_op jit(solution)/shard_map/all_to_all | solution.py:15
  42.4 70.8 %all-gather.2.cloned.1.call-start = ((), (), s32[]{:S(2)}) async-start(), calls=%async_computation.4 | async-start | bytes 2359296 | tf_op jit(solution)/shard_map/all_gather | solution.py:43
  58.7 57.7 %all-to-all-start.1 = ((bf16[8,64,2048]{2,1,0:T(8,128)(2,1)}), bf16[8,64,2048]{2,1,0:T(8,128)(2,1)S(1)}, u32[]{:S(2)}, u32[]{:S(2)}) async-start(bf16[8,64,2048]{2,1,0:T(8,128)(2,1)} %stack.3), calls=%async_computation.1 | async-start | bytes 4194304 | tf_op jit(solution)/shard_map/all_to_all | solution.py:38
Sparse Core Ops, SparseCore 0:
  57.2 55.9 all-gather.1
